TPU v7x, 32 devices: a whole 2x2x4 slice. The times are simulated.
32 devices in a mesh: grp: 2 (over x), ctx: 16 (over z, y, core).
Axes of the slice: x: 2, y: 2, z: 4, core: 2. Of those that a mesh axis runs over, the one named last changes fastest.
Arguments:
- cache_keys: bfloat16 [2048, 512], P(('grp', 'ctx')), parts along dimension 0, may hold values from -4 to 4
- cache_values: bfloat16 [2048, 512], P(('grp', 'ctx')), parts along dimension 0, may hold values from -4 to 4
- new_queries: bfloat16 [2048, 4096], P(('grp', 'ctx')), parts along dimension 0, may hold values from -600 to 600
- new_keys: bfloat16 [2048, 512], P(('grp', 'ctx')), parts along dimension 0, may hold values from -4 to 4
- new_values: bfloat16 [2048, 512], P(('grp', 'ctx')), parts along dimension 0, may hold values from -4 to 4
- cont_queries: bfloat16 [64, 4096], P(('grp', 'ctx')), parts along dimension 0, may hold values from -600 to 600
- suffix_keys: bfloat16 [64, 128, 512], P(('grp', 'ctx')), parts along dimension 0, may hold values from -4 to 4
- suffix_values: bfloat16 [64, 128, 512], P(('grp', 'ctx')), parts along dimension 0, may hold values from -4 to 4
- window_start: int32 [2], P('grp'), parts along dimension 0, may hold values from 0 to 255
- prefix_length: int32 [2], P('grp'), parts along dimension 0, may hold values from 512 to 1024
- suffix_length: int32 [64], P(('grp', 'ctx')), parts along dimension 0, may hold values from 2 to 128
Outputs:
- prompt_out: bfloat16 [2048, 4096], P(('grp', 'ctx')), parts along dimension 0
- cont_out: bfloat16 [64, 4096], P(('grp', 'ctx')), parts along dimension 0
There are 2 independent parts, one for each index of `grp`. A program takes and returns all parts, laid end to end along the dimension named above; each array names one. Nothing has to cross between parts.
All inputs are finite; a program needn't handle non-finite values.
Results may differ from a plain program's by a relative error of at most 0.009.
Values may be sent and summed in bfloat16 or wider, within the bound.
No kernel may reach another device: no remote copies, remote signals or barrier semaphores. Data moves between devices by JAX's collectives and lax.ppermute only.
A program may use at most 192 MiB of HBM per device.

v0:
```python
import jax
import jax.numpy as jnp
from jax import lax
from jax.sharding import PartitionSpec as P

KVH = 4
HD = 128
GROUP = 8


def empty_running(row_count):
    return (
        jnp.full((row_count, KVH, GROUP), -1e30, jnp.float32),
        jnp.zeros((row_count, KVH, GROUP), jnp.float32),
        jnp.zeros((row_count, KVH, GROUP, HD), jnp.float32),
    )


def key_places(begin_row, row_count, cache_rows, prompt_rows, window_first, prefix_last):
    position = begin_row + jnp.arange(row_count, dtype=jnp.int32)
    stride = cache_rows + prompt_rows
    shard_index = position // stride
    within = position % stride
    in_cache = within < cache_rows
    cache_index = shard_index * cache_rows + within
    prompt_index = shard_index * prompt_rows + within - cache_rows
    cache_ok = in_cache & (cache_index >= window_first) & (cache_index < prefix_last)
    return (in_cache, cache_ok, prompt_index)


def attend_piece(running, queries, visible, key_piece, value_piece):
    row_max, row_sum, numerator = running
    count = key_piece.shape[0]
    key_heads = key_piece.reshape(count, KVH, HD)
    value_heads = value_piece.reshape(count, KVH, HD)
    scores = jnp.einsum(
        "rkgd,lkd->rkgl", queries, key_heads, preferred_element_type=jnp.float32
    ) * HD ** (-0.5)
    mask = visible[:, None, None, :]
    scores = jnp.where(mask, scores, -1e30)
    new_max = jnp.maximum(row_max, jnp.max(scores, axis=-1))
    probs = jnp.where(mask, jnp.exp(scores - new_max[..., None]), 0.0)
    row_sum = jnp.sum(probs, axis=-1)
    numerator = jnp.einsum(
        "rkgl,lkd->rkgd",
        probs.astype(jnp.bfloat16),
        value_heads,
        preferred_element_type=jnp.float32,
    )
    return (new_max, row_sum, numerator)


def combine_states(stacked, suffix_state):
    stack_max, stack_sum, stack_numer = stacked
    suffix_max, suffix_sum, suffix_numer = suffix_state
    highest = jnp.maximum(jnp.max(stack_max, axis=0), suffix_max)
    stack_weight = jnp.exp(stack_max - highest)
    suffix_weight = jnp.exp(suffix_max - highest)
    numerator = (
        jnp.sum(stack_numer * stack_weight[..., None], axis=0)
        + suffix_numer * suffix_weight[..., None]
    )
    denominator = jnp.sum(stack_sum * stack_weight, axis=0) + suffix_sum * suffix_weight
    return numerator / denominator[..., None]


def body(
    cache_keys,
    cache_values,
    new_queries,
    new_keys,
    new_values,
    cont_queries,
    suffix_keys,
    suffix_values,
    window_start,
    prefix_length,
    suffix_length,
):
    cache_rows = cache_keys.shape[0]
    prompt_rows = new_keys.shape[0]
    window_first = window_start[0]
    prefix_last = prefix_length[0]
    device_place = lax.axis_index("ctx")
    query_index = device_place * prompt_rows + jnp.arange(prompt_rows, dtype=jnp.int32)
    prompt_heads = new_queries.reshape(prompt_rows, KVH, GROUP, HD)
    local_keys = jnp.concatenate([cache_keys, new_keys], axis=0)
    local_values = jnp.concatenate([cache_values, new_values], axis=0)
    cont_count = cont_queries.shape[0]
    cont_heads = cont_queries.reshape(cont_count, KVH, GROUP, HD)
    suffix_rows = suffix_keys.shape[1]
    own_keys = suffix_keys.reshape(cont_count, suffix_rows, KVH, HD)
    own_values = suffix_values.reshape(cont_count, suffix_rows, KVH, HD)
    suffix_scores = jnp.einsum(
        "ckgd,cskd->ckgs", cont_heads, own_keys, preferred_element_type=jnp.float32
    ) * HD ** (-0.5)
    suffix_mask = (jnp.arange(suffix_rows, dtype=jnp.int32)[None, :] < suffix_length[:, None])[
        :, None, None, :
    ]
    suffix_scores = jnp.where(suffix_mask, suffix_scores, -1e30)
    suffix_max = jnp.max(suffix_scores, axis=-1)
    suffix_probs = jnp.where(suffix_mask, jnp.exp(suffix_scores - suffix_max[..., None]), 0.0)
    suffix_sum = jnp.sum(suffix_probs, axis=-1)
    suffix_numer = jnp.einsum(
        "ckgs,cskd->ckgd",
        suffix_probs.astype(jnp.bfloat16),
        own_values,
        preferred_element_type=jnp.float32,
    )
    suffix_state = (suffix_max, suffix_sum, suffix_numer)
    key_piece = lax.all_gather(local_keys, "ctx", axis=0, tiled=True)
    in_cache, cache_ok, prompt_index = key_places(
        jnp.int32(0), key_piece.shape[0], cache_rows, prompt_rows, window_first, prefix_last
    )
    visible = cache_ok[None, :] | (~in_cache)[None, :] & (
        prompt_index[None, :] <= query_index[:, None]
    )
    prompt_state = attend_piece(
        empty_running(prompt_rows),
        prompt_heads,
        visible,
        key_piece,
        lax.all_gather(local_values, "ctx", axis=0, tiled=True),
    )
    every_query = lax.all_gather(cont_queries, "ctx", axis=0, tiled=True)
    every_count = every_query.shape[0]
    every_heads = every_query.reshape(every_count, KVH, GROUP, HD)
    in_cache, cache_ok, prompt_index = key_places(
        device_place * (cache_rows + prompt_rows),
        local_keys.shape[0],
        cache_rows,
        prompt_rows,
        window_first,
        prefix_last,
    )
    visible = (cache_ok | ~in_cache)[None, :]
    local_max, local_sum, local_numer = attend_piece(
        empty_running(every_count), every_heads, visible, local_keys, local_values
    )
    exchanged = (
        lax.all_to_all(local_numer[None], "ctx", split_axis=1, concat_axis=0, tiled=True),
        lax.all_to_all(local_max[None], "ctx", split_axis=1, concat_axis=0, tiled=True),
        lax.all_to_all(local_sum[None], "ctx", split_axis=1, concat_axis=0, tiled=True),
    )
    stacked = (exchanged[1], exchanged[2], exchanged[0])
    prompt_max, prompt_sum, prompt_numer = prompt_state
    prompt_out = (
        (prompt_numer / prompt_sum[..., None])
        .reshape(prompt_rows, new_queries.shape[1])
        .astype(jnp.bfloat16)
    )
    cont_out = (
        combine_states(stacked, suffix_state)
        .reshape(cont_count, cont_queries.shape[1])
        .astype(jnp.bfloat16)
    )
    return (prompt_out, cont_out)


def solution(mesh):
    in_specs = (
        P(("grp", "ctx"), None),
        P(("grp", "ctx"), None),
        P(("grp", "ctx"), None),
        P(("grp", "ctx"), None),
        P(("grp", "ctx"), None),
        P(("grp", "ctx"), None),
        P(("grp", "ctx"), None, None),
        P(("grp", "ctx"), None, None),
        P("grp"),
        P("grp"),
        P(("grp", "ctx")),
    )
    out_specs = (P(("grp", "ctx"), None), P(("grp", "ctx"), None))
    return jax.shard_map(body, mesh=mesh, in_specs=in_specs, out_specs=out_specs, check_vma=False)
```

profile of v0, /device:TPU:0, one launch (start us, length us, event | category | flops | bytes accessed | tf_op | source)
XLA Modules:
  0.0 118.5 jit_solution(2128454379710857456)
XLA Ops:
  7.2 1.0 copy.85
  8.2 1.0 copy.86
  9.2 0.8 pad_maximum_fusion.1
  11.3 24.1 %all-gather = bf16[16,2,4096]{2,1,0:T(2,128)(2,1)S(1)} all-gather(bf16[1,2,4096]{2,1,0:T(2,128)(2,1)} %bitcast.110), channel_id=1, replica_groups=mesh['grp'=2,'ctx'=16] {'ctx'}, dimensions={0}, use_global_device_ids=true | all-gather | bytes 278528 | tf_op jit(solution)/shard_map/all_gather | solution.py:125
  35.7 1.3 %fusion.56 = (f32[32,4,8]{0,2,1:T(8,128)S(1)}, f32[32,4,8,128]{3,0,2,1:T(8,128)S(1)}) fusion(bf16[128,4,128,1]{0,2,3,1:T(8,128)(2,1)} %bitcast.103, bf16[32,4,8,128]{3,2,1,0:T(8,128)(2,1)S(1)} %reshape.240, pred[128]{0:T(512)(128)(4,1)S(1)} %not_or_fusion), kind=kOutput, calls=%fused_computation.85 | convolution fusion | flops 33946624 | bytes 921728 | tf_op jit(solution)/shard_map/rkgd,lkd->rkgl/dot_general | solution.py:36
  37.0 0.4 fusion.21
  37.3 0.7 copy.104
  38.1 3.5 %all-to-all-start.2 = ((f32[1,32,4,8]{3,2,0,1:T(4,128)}), f32[1,32,4,8]{3,2,0,1:T(4,128)S(1)}, u32[]{:S(2)}, u32[]{:S(2)}) async-start(f32[1,32,4,8]{3,2,0,1:T(4,128)} %copy.104), calls=%async_computation.2 | async-start | bytes 131072 | tf_op jit(solution)/shard_map/all_to_all | solution.py:143
  41.6 1.0 copy.83
  42.6 1.0 copy.84
  43.5 0.8 pad_maximum_fusion
  44.3 0.7 iota_compare_fusion
  45.1 1.2 %convolution_bitcast_fusion = f32[1,32,4,8,128]{4,1,3,2,0:T(8,128)S(1)} fusion(bf16[128,4,128,1]{0,2,3,1:T(8,128)(2,1)} %bitcast.104, f32[32,4,8,128]{3,0,2,1:T(8,128)S(1)} %get-tuple-element.11, f32[32,4,8]{0,2,1:T(8,128)S(1)} %get-tuple-element.7, pred[128]{0:T(512)(128)(4,1)S(1)} %not_or_fusion), kind=kOutput, calls=%fused_computation.8 | convolution fusion | flops 33947648 | bytes 1183872 | tf_op jit(solution)/shard_map/rkgl,lkd->rkgd/dot_general | solution.py:44
  46.3 1.1 fusion.57
  47.6 0.7 copy.95
  48.3 1.3 %all-to-all-done.2 = f32[1,32,4,8]{3,2,0,1:T(4,128)S(1)} async-done(((f32[1,32,4,8]{3,2,0,1:T(4,128)}), f32[1,32,4,8]{3,2,0,1:T(4,128)S(1)}, u32[]{:S(2)}, u32[]{:S(2)}) %all-to-all-start.2) | async-done | bytes 4128 | tf_op jit(solution)/shard_map/all_to_all | solution.py:143
  49.5 4.7 %all-to-all-start.1 = ((f32[1,32,4,8]{3,2,0,1:T(4,128)}), f32[1,32,4,8]{3,2,0,1:T(4,128)S(1)}, u32[]{:S(2)}, u32[]{:S(2)}) async-start(f32[1,32,4,8]{3,2,0,1:T(4,128)} %copy.95), calls=%async_computation.1 | async-start | bytes 131072 | tf_op jit(solution)/shard_map/all_to_all | solution.py:142
  54.2 1.1 copy.94
  55.3 1.1 copy.121
  56.5 4.6 %all-to-all-done.1 = f32[1,32,4,8]{3,2,0,1:T(4,128)S(1)} async-done(((f32[1,32,4,8]{3,2,0,1:T(4,128)}), f32[1,32,4,8]{3,2,0,1:T(4,128)S(1)}, u32[]{:S(2)}, u32[]{:S(2)}) %all-to-all-start.1) | async-done | bytes 4128 | tf_op jit(solution)/shard_map/all_to_all | solution.py:142
  61.1 3.6 %all-to-all-start = ((f32[1,32,4,8,128]{4,3,2,0,1:T(8,128)}), f32[1,32,4,8,128]{4,3,2,0,1:T(8,128)S(1)}, u32[]{:S(2)}, u32[]{:S(2)}) async-start(f32[1,32,4,8,128]{4,3,2,0,1:T(8,128)} %copy.94), calls=%async_computation | async-start | bytes 1048576 | tf_op jit(solution)/shard_map/all_to_all | solution.py:141
  65.1 0.5 copy.100
  65.5 16.9 %all-to-all-done = f32[1,32,4,8,128]{4,3,2,0,1:T(8,128)S(1)} async-done(((f32[1,32,4,8,128]{4,3,2,0,1:T(8,128)}), f32[1,32,4,8,128]{4,3,2,0,1:T(8,128)S(1)}, u32[]{:S(2)}, u32[]{:S(2)}) %all-to-all-start) | async-done | bytes 524320 | tf_op jit(solution)/shard_map/all_to_all | solution.py:141
  82.4 0.7 fusion.18
  83.1 1.2 %fusion.15 = bf16[1,2,32,128]{3,2,1,0:T(8,128)(2,1)S(1)} fusion(f32[2,4,8,128]{3,0,2,1:T(2,128)S(1)} %fusion.18, f32[2,4,8,128]{3,2,1,0:T(8,128)S(1)} %get-tuple-element.13, f32[2,4,8]{2,1,0:T(4,128)S(1)} %get-tuple-element.2, f32[2,4,8]{2,1,0:T(4,128)S(1)} %get-tuple-element.3, f32[2,4,8]{2,1,0:T(4,128)S(1)} %get-tuple-element.12, ...), kind=kOutput, calls=%fused_computation.18 | convolution fusion | flops 2154496 | bytes 345088 | tf_op jit(solution)/shard_map/ckgs,cskd->ckgd/dot_general | solution.py:104
  84.3 0.6 copy.161
  85.0 4.6 %fusion = (f32[64,4,8]{0,2,1:T(8,128)S(1)}, f32[4,2048,64,8]{1,2,3,0:T(8,128)S(1)}) fusion(pred[64,2048]{1,0:T(8,128)(4,1)S(1)} %and_or_fusion, bf16[2048,4,128,1]{0,2,3,1:T(8,128)(2,1)} %bitcast.102, bf16[64,4,8,128]{3,2,1,0:T(8,128)(2,1)S(1)} %bitcast.99), kind=kOutput, calls=%fused_computation.2 | convolution fusion | flops 1086322688 | bytes 19537920 | tf_op jit(solution)/shard_map/rkgd,lkd->rkgl/dot_general | solution.py:36
  89.6 5.7 %copy-done.1 = f32[4,2048,64,8]{1,2,3,0:T(8,128)} copy-done((f32[4,2048,64,8]{1,2,3,0:T(8,128)}, f32[4,2048,64,8]{1,2,3,0:T(8,128)S(1)}, u32[]{:S(2)}) %copy-start.1) | copy-done | bytes 16777240
  95.3 5.1 %fusion.1 = f32[64,4,8]{0,2,1:T(8,128)S(1)} fusion(f32[4,2048,64,8]{1,2,3,0:T(8,128)S(1)} %get-tuple-element.9, f32[64,4,8]{0,2,1:T(8,128)S(1)} %broadcast_maximum_fusion.1, pred[64,2048]{1,0:T(8,128)(4,1)S(1)} %and_or_fusion), kind=kLoop, calls=%fused_computation.3 | loop fusion | flops 20969472 | bytes 16924672 | tf_op jit(solution)/shard_map/reduce_sum | solution.py:43
  100.4 1.6 %all-gather.4.cloned.1.call-done = bf16[2048,512]{0,1:T(8,128)(2,1)} async-done(((bf16[128,512]{0,1:T(8,128)(2,1)}), bf16[2048,512]{0,1:T(8,128)(2,1)}) %all-gather.4.cloned.1.call-update) | async-done | bytes 2097168 | tf_op jit(solution)/shard_map/all_gather | solution.py:123
  102.0 8.3 %divide_convert_fusion = bf16[64,4,8,128]{3,0,2,1:T(8,128)(2,1)S(1)} fusion(bf16[2048,4,128,1]{0,2,3,1:T(8,128)(2,1)} %bitcast.114, f32[4,2048,64,8]{1,2,3,0:T(8,128)} %copy-done.1, f32[64,4,8]{0,2,1:T(8,128)S(1)} %broadcast_maximum_fusion.1, pred[64,2048]{1,0:T(8,128)(4,1)S(1)} %and_or_fusion, f32[64,4,8]{0,2,1:T(8,128)S(1)} %fusion.1), kind=kOutput, calls=%fused_computation.19 | convolution fusion | flops 1095237632 | bytes 19546112 | tf_op jit(solution)/shard_map/rkgl,lkd->rkgd/dot_general | solution.py:44
  110.7 1.0 copy.160
  (25 shorter events, 1.2 us)
Async XLA Ops:
  7.2 39.1 %copy-start = (bf16[2,128,512]{2,1,0:T(8,128)(2,1)S(1)}, bf16[2,128,512]{2,1,0:T(8,128)(2,1)}, u32[]{:S(2)}) copy-start(bf16[2,128,512]{2,1,0:T(8,128)(2,1)} %param.17) | copy-start | bytes 786436
  7.2 77.8 %all-gather.6.cloned.1.call-start = ((), (), s32[]{:S(2)}) async-start(), calls=%async_computation.4 | async-start | bytes 2228224 | tf_op jit(solution)/shard_map/all_gather | solution.py:111
  38.1 11.5 %all-to-all-start.2 = ((f32[1,32,4,8]{3,2,0,1:T(4,128)}), f32[1,32,4,8]{3,2,0,1:T(4,128)S(1)}, u32[]{:S(2)}, u32[]{:S(2)}) async-start(f32[1,32,4,8]{3,2,0,1:T(4,128)} %copy.104), calls=%async_computation.2 | async-start | bytes 131072 | tf_op jit(solution)/shard_map/all_to_all | solution.py:143
  41.6 60.4 %all-gather.4.cloned.1.call-start = ((), (), s32[]{:S(2)}) async-start(), calls=%async_computation.3 | async-start | bytes 2228224 | tf_op jit(solution)/shard_map/all_gather | solution.py:123
  49.5 11.6 %all-to-all-start.1 = ((f32[1,32,4,8]{3,2,0,1:T(4,128)}), f32[1,32,4,8]{3,2,0,1:T(4,128)S(1)}, u32[]{:S(2)}, u32[]{:S(2)}) async-start(f32[1,32,4,8]{3,2,0,1:T(4,128)} %copy.95), calls=%async_computation.1 | async-start | bytes 131072 | tf_op jit(solution)/shard_map/all_to_all | solution.py:142
  61.1 21.3 %all-to-all-start = ((f32[1,32,4,8,128]{4,3,2,0,1:T(8,128)}), f32[1,32,4,8,128]{4,3,2,0,1:T(8,128)S(1)}, u32[]{:S(2)}, u32[]{:S(2)}) async-start(f32[1,32,4,8,128]{4,3,2,0,1:T(8,128)} %copy.94), calls=%async_computation | async-start | bytes 1048576 | tf_op jit(solution)/shard_map/all_to_all | solution.py:141
  89.6 5.7 %copy-start.1 = (f32[4,2048,64,8]{1,2,3,0:T(8,128)}, f32[4,2048,64,8]{1,2,3,0:T(8,128)S(1)}, u32[]{:S(2)}) copy-start(f32[4,2048,64,8]{1,2,3,0:T(8,128)S(1)} %get-tuple-element.9) | copy-start | bytes 50331652
Sparse Core Ops, SparseCore 0:
  10.1 44.8 all-gather.5
  57.2 44.6 all-gather.3
where the time goes:
time: 119 us
  waiting for transfers between devices  24.4 us (21%)
  blocking collectives  24.1 us (20%)
  matrix products  17.7 us (15%)
  local copies, waits for them, and re-layouts  15.9 us (13%)
  between operations  15.6 us (13%)
  starting transfers between devices  11.8 us (10%)
  other arithmetic  8.98 us (8%)
    all_gather x1, blocking collectives, body(): every_query = lax.all_gather(cont_queries, 'ctx', axis=0, tiled=True)  24.1 us
    all_to_all x1, waiting for transfers between devices, body(): lax.all_to_all(local_numer[None], 'ctx', split_axis=1, concat_axis=0, til...  16.9 us
    unnamed x11, local copies, waits for them, and re-layouts  12.3 us
    dot_general x2, matrix products, attend_piece(): jnp.einsum('rkgl,lkd->rkgd', probs.astype(jnp.bfloat16), value_heads, pre...  9.58 us
    dot_general x2, matrix products, attend_piece(): jnp.einsum('rkgd,lkd->rkgl', queries, key_heads, preferred_element_type=j...  5.89 us
    reduce_sum x2, other arithmetic, attend_piece(): row_sum = jnp.sum(probs, axis=-1)  5.49 us
    all_to_all x1, starting transfers between devices, body(): lax.all_to_all(local_max[None], 'ctx', split_axis=1, concat_axis=0, tiled...  4.68 us
    all_to_all x1, waiting for transfers between devices, body(): lax.all_to_all(local_max[None], 'ctx', split_axis=1, concat_axis=0, tiled...  4.64 us
  transfers between devices with their start and end apart: 5, of which 4 were waited for; matrix products, arithmetic and copies ran while one was open for 21% of the time, Pallas kernels for 0%

commit v1 on v0

--- a/solution.py
+++ b/solution.py
@@ -6,6 +6,13 @@
 KVH = 4
 HD = 128
 GROUP = 8
+
+
+def stacked_exchange(x, mesh_axis, split, join):
+    peers = lax.axis_size(mesh_axis)
+    shards = jnp.stack(jnp.split(x, peers, axis=split), axis=0)
+    shards = lax.all_to_all(shards, mesh_axis, split_axis=0, concat_axis=0)
+    return jnp.concatenate(shards, axis=join)
 
 
 def empty_running(row_count):
@@ -139,7 +146,7 @@
     )
     exchanged = (
         lax.all_to_all(local_numer[None], "ctx", split_axis=1, concat_axis=0, tiled=True),
-        lax.all_to_all(local_max[None], "ctx", split_axis=1, concat_axis=0, tiled=True),
+        stacked_exchange(local_max[None], "ctx", 1, 0),
         lax.all_to_all(local_sum[None], "ctx", split_axis=1, concat_axis=0, tiled=True),
     )
     stacked = (exchanged[1], exchanged[2], exchanged[0])

time: 119 us -> 129 us (1.084)
  local copies, waits for them, and re-layouts: 15.9 us -> 26.3 us
  waiting for transfers between devices: 24.4 us -> 22.6 us
  starting transfers between devices: 11.8 us -> 13.1 us
    unnamed x11 -> x26, local copies, waits for them, and re-layouts: 12.3 us -> 21.3 us
    all_to_all x1, waiting for transfers between devices: 4.64 us -> 0.01 us  [stacked_exchange(): shards = lax.all_to_all(shards, mesh_axis, split_axis=0, concat_axis=0)]
    all_to_all x1, waiting for transfers between devices: 1.29 us -> 4.85 us  [body(): lax.all_to_all(local_sum[None], 'ctx', split_axis=1, concat_axis=0, tiled...]
    all_to_all x1, starting transfers between devices: 3.5 us -> 5.97 us  [body(): lax.all_to_all(local_sum[None], 'ctx', split_axis=1, concat_axis=0, tiled...]
    split x0 -> x17, local copies, waits for them, and re-layouts: none -> 1.68 us  [stacked_exchange(): shards = jnp.stack(jnp.split(x, peers, axis=split), axis=0)]
    all_gather x1, waiting for transfers between devices: 1.55 us -> 0.01 us  [body(): lax.all_gather(local_values, 'ctx', axis=0, tiled=True)]
  transfers between devices with their start and end apart: 5 -> 5, of which waited for: 4 -> 2; matrix products, arithmetic and copies ran while one was open for 21% -> 27% of each run, Pallas kernels for 0% -> 0%
where the time goes in v1:
time: 129 us; the launch traced here: 128 us
  local copies, waits for them, and re-layouts  26.3 us (20%)
  blocking collectives  24.1 us (19%)
  waiting for transfers between devices  22.6 us (18%)
  matrix products  17.5 us (14%)
  between operations  15.5 us (12%)
  starting transfers between devices  13.1 us (10%)
  other arithmetic  8.98 us (7%)
    all_gather x1, blocking collectives, body(): every_query = lax.all_gather(cont_queries, 'ctx', axis=0, tiled=True)  24.1 us
    unnamed x26, local copies, waits for them, and re-layouts  21.3 us
    all_to_all x1, waiting for transfers between devices, body(): lax.all_to_all(local_numer[None], 'ctx', split_axis=1, concat_axis=0, til...  17.7 us
    dot_general x2, matrix products, attend_piece(): jnp.einsum('rkgl,lkd->rkgd', probs.astype(jnp.bfloat16), value_heads, pre...  9.59 us
    all_to_all x1, starting transfers between devices, body(): lax.all_to_all(local_sum[None], 'ctx', split_axis=1, concat_axis=0, tiled...  5.97 us
    dot_general x2, matrix products, attend_piece(): jnp.einsum('rkgd,lkd->rkgl', queries, key_heads, preferred_element_type=j...  5.7 us
    reduce_sum x2, other arithmetic, attend_piece(): row_sum = jnp.sum(probs, axis=-1)  5.48 us
    all_to_all x1, waiting for transfers between devices, body(): lax.all_to_all(local_sum[None], 'ctx', split_axis=1, concat_axis=0, tiled...  4.85 us
  transfers between devices with their start and end apart: 5, of which 2 were waited for; matrix products, arithmetic and copies ran while one was open for 27% of the time, Pallas kernels for 0%

profile of v1, /device:TPU:0, one launch (start us, length us, event | category | flops | bytes accessed | tf_op | source)
XLA Modules:
  0.0 128.2 jit_solution(10867136808076851067)
XLA Ops:
  7.2 1.0 copy.35
  8.2 1.0 copy.36
  9.2 0.8 pad_maximum_fusion.1
  11.3 24.1 %all-gather = bf16[16,2,4096]{2,1,0:T(2,128)(2,1)S(1)} all-gather(bf16[1,2,4096]{2,1,0:T(2,128)(2,1)} %bitcast.151), channel_id=1, replica_groups=mesh['grp'=2,'ctx'=16] {'ctx'}, dimensions={0}, use_global_device_ids=true | all-gather | bytes 278528 | tf_op jit(solution)/shard_map/all_gather | solution.py:132
  35.7 1.3 fusion.59
  38.6 0.6 constant_dynamic-update-slice_fusion.15
  39.3 0.6 constant_dynamic-update-slice_fusion.14
  39.9 0.6 constant_dynamic-update-slice_fusion.13
  40.4 0.6 constant_dynamic-update-slice_fusion.12
  41.0 0.6 constant_dynamic-update-slice_fusion.11
  48.2 3.5 %all-to-all-start.1 = ((f32[16,1,2,4,8]{4,3,2,1,0:T(4,128)}), f32[16,1,2,4,8]{4,3,2,1,0:T(4,128)S(1)}, u32[]{:S(2)}, u32[]{:S(2)}) async-start(f32[16,1,2,4,8]{4,3,2,1,0:T(4,128)} %constant_dynamic-update-slice_fusion), calls=%async_computation.1 | async-start | bytes 131072 | tf_op jit(solution)/shard_map/all_to_all | solution.py:14
  51.7 1.0 copy.33
  52.7 1.0 copy.34
  53.7 0.8 pad_maximum_fusion
  54.4 0.7 iota_compare_fusion
  55.6 1.2 convolution_bitcast_fusion
  56.8 1.0 fusion.60
  58.0 0.7 copy.66
  58.7 6.0 %all-to-all-start.2 = ((f32[1,32,4,8]{3,2,0,1:T(4,128)}), f32[1,32,4,8]{3,2,0,1:T(4,128)S(1)}, u32[]{:S(2)}, u32[]{:S(2)}) async-start(f32[1,32,4,8]{3,2,0,1:T(4,128)} %copy.66), calls=%async_computation.2 | async-start | bytes 131072 | tf_op jit(solution)/shard_map/all_to_all | solution.py:150
  64.7 1.1 copy.44
  65.8 1.1 copy.81
  67.0 4.9 %all-to-all-done.2 = f32[1,32,4,8]{3,2,0,1:T(4,128)S(1)} async-done(((f32[1,32,4,8]{3,2,0,1:T(4,128)}), f32[1,32,4,8]{3,2,0,1:T(4,128)S(1)}, u32[]{:S(2)}, u32[]{:S(2)}) %all-to-all-start.2) | async-done | bytes 4128 | tf_op jit(solution)/shard_map/all_to_all | solution.py:150
  71.8 3.6 %all-to-all-start = ((f32[1,32,4,8,128]{4,3,2,0,1:T(8,128)}), f32[1,32,4,8,128]{4,3,2,0,1:T(8,128)S(1)}, u32[]{:S(2)}, u32[]{:S(2)}) async-start(f32[1,32,4,8,128]{4,3,2,0,1:T(8,128)} %copy.44), calls=%async_computation | async-start | bytes 1048576 | tf_op jit(solution)/shard_map/all_to_all | solution.py:148
  76.2 17.7 %all-to-all-done = f32[1,32,4,8,128]{4,3,2,0,1:T(8,128)S(1)} async-done(((f32[1,32,4,8,128]{4,3,2,0,1:T(8,128)}), f32[1,32,4,8,128]{4,3,2,0,1:T(8,128)S(1)}, u32[]{:S(2)}, u32[]{:S(2)}) %all-to-all-start) | async-done | bytes 524320 | tf_op jit(solution)/shard_map/all_to_all | solution.py:148
  93.9 0.7 fusion.18
  94.6 1.2 fusion.15
  95.8 0.6 copy.116
  96.4 4.4 %fusion = (f32[64,4,8]{0,2,1:T(8,128)S(1)}, f32[4,2048,64,8]{1,2,3,0:T(8,128)S(1)}) fusion(pred[64,2048]{1,0:T(8,128)(4,1)S(1)} %and_or_fusion, bf16[2048,4,128,1]{0,2,3,1:T(8,128)(2,1)} %bitcast.144, bf16[64,4,8,128]{3,2,1,0:T(8,128)(2,1)S(1)} %bitcast.141), kind=kOutput, calls=%fused_computation.2 | convolution fusion | flops 1086322688 | bytes 19537920 | tf_op jit(solution)/shard_map/rkgd,lkd->rkgl/dot_general | solution.py:43
  100.9 5.7 %copy-done.1 = f32[4,2048,64,8]{1,2,3,0:T(8,128)} copy-done((f32[4,2048,64,8]{1,2,3,0:T(8,128)}, f32[4,2048,64,8]{1,2,3,0:T(8,128)S(1)}, u32[]{:S(2)}) %copy-start.1) | copy-done | bytes 16777240
  106.6 5.1 %fusion.1 = f32[64,4,8]{0,2,1:T(8,128)S(1)} fusion(f32[4,2048,64,8]{1,2,3,0:T(8,128)S(1)} %get-tuple-element.25, f32[64,4,8]{0,2,1:T(8,128)S(1)} %broadcast_maximum_fusion.1, pred[64,2048]{1,0:T(8,128)(4,1)S(1)} %and_or_fusion), kind=kLoop, calls=%fused_computation.3 | loop fusion | flops 20969472 | bytes 16924672 | tf_op jit(solution)/shard_map/reduce_sum | solution.py:50
  111.7 8.4 %divide_convert_fusion = bf16[64,4,8,128]{3,0,2,1:T(8,128)(2,1)S(1)} fusion(bf16[2048,4,128,1]{0,2,3,1:T(8,128)(2,1)} %bitcast.160, f32[4,2048,64,8]{1,2,3,0:T(8,128)} %copy-done.1, f32[64,4,8]{0,2,1:T(8,128)S(1)} %broadcast_maximum_fusion.1, pred[64,2048]{1,0:T(8,128)(4,1)S(1)} %and_or_fusion, f32[64,4,8]{0,2,1:T(8,128)S(1)} %fusion.1), kind=kOutput, calls=%fused_computation.19 | convolution fusion | flops 1095237632 | bytes 19546112 | tf_op jit(solution)/shard_map/rkgl,lkd->rkgd/dot_general | solution.py:51
  120.4 1.0 copy.115
  (54 shorter events, 10.2 us)
Async XLA Ops:
  7.2 49.6 %copy-start = (bf16[2,128,512]{2,1,0:T(8,128)(2,1)S(1)}, bf16[2,128,512]{2,1,0:T(8,128)(2,1)}, u32[]{:S(2)}) copy-start(bf16[2,128,512]{2,1,0:T(8,128)(2,1)} %param.17) | copy-start | bytes 786436
  7.2 89.2 %all-gather.6.cloned.1.call-start = ((), (), s32[]{:S(2)}) async-start(), calls=%async_computation.4 | async-start | bytes 2228224 | tf_op jit(solution)/shard_map/all_gather | solution.py:118
  48.2 10.6 %all-to-all-start.1 = ((f32[16,1,2,4,8]{4,3,2,1,0:T(4,128)}), f32[16,1,2,4,8]{4,3,2,1,0:T(4,128)S(1)}, u32[]{:S(2)}, u32[]{:S(2)}) async-start(f32[16,1,2,4,8]{4,3,2,1,0:T(4,128)} %constant_dynamic-update-slice_fusion), calls=%async_computation.1 | async-start | bytes 131072 | tf_op jit(solution)/shard_map/all_to_all | solution.py:14
  51.7 60.0 %all-gather.4.cloned.1.call-start = ((), (), s32[]{:S(2)}) async-start(), calls=%async_computation.3 | async-start | bytes 2228224 | tf_op jit(solution)/shard_map/all_gather | solution.py:130
  58.7 13.1 %all-to-all-start.2 = ((f32[1,32,4,8]{3,2,0,1:T(4,128)}), f32[1,32,4,8]{3,2,0,1:T(4,128)S(1)}, u32[]{:S(2)}, u32[]{:S(2)}) async-start(f32[1,32,4,8]{3,2,0,1:T(4,128)} %copy.66), calls=%async_computation.2 | async-start | bytes 131072 | tf_op jit(solution)/shard_map/all_to_all | solution.py:150
  71.8 22.0 %all-to-all-start = ((f32[1,32,4,8,128]{4,3,2,0,1:T(8,128)}), f32[1,32,4,8,128]{4,3,2,0,1:T(8,128)S(1)}, u32[]{:S(2)}, u32[]{:S(2)}) async-start(f32[1,32,4,8,128]{4,3,2,0,1:T(8,128)} %copy.44), calls=%async_computation | async-start | bytes 1048576 | tf_op jit(solution)/shard_map/all_to_all | solution.py:148
  100.8 5.7 %copy-start.1 = (f32[4,2048,64,8]{1,2,3,0:T(8,128)}, f32[4,2048,64,8]{1,2,3,0:T(8,128)S(1)}, u32[]{:S(2)}) copy-start(f32[4,2048,64,8]{1,2,3,0:T(8,128)S(1)} %get-tuple-element.25) | copy-start | bytes 50331652
Sparse Core Ops, SparseCore 0:
  10.1 44.1 all-gather.5
  56.5 45.3 all-gather.3
